TPU v7x, 512 devices: a whole 4x8x8 slice. The times are simulated.
512 devices in a mesh: ctx: 32 (over z_hi, y, core), tp: 16 (over z_lo, x).
Axes of the slice: x: 4, y: 8, z: 8 (z_hi: 2, z_lo: 4; z = z_hi * 4 + z_lo), core: 2. Of those that a mesh axis runs over, the one named last changes fastest.
Arguments:
- enc_query: bfloat16 [5120, 6144], P(('ctx', 'tp')), may hold values from -40 to 40
- enc_key: bfloat16 [5120, 6144], P(('ctx', 'tp')), may hold values from -5 to 5
- enc_value: bfloat16 [5120, 6144], P(('ctx', 'tp')), may hold values from -6 to 6
- dec_query: bfloat16 [1024, 6144], P(('ctx', 'tp')), may hold values from -40 to 40
- cross_key: bfloat16 [5120, 6144], P(('ctx', 'tp')), may hold values from -5 to 5
- cross_value: bfloat16 [5120, 6144], P(('ctx', 'tp')), may hold values from -6 to 6
Outputs:
- enc_context: bfloat16 [5120, 6144], P('ctx', 'tp')
- dec_context: bfloat16 [1024, 6144], P('ctx', 'tp')
All inputs are finite; a program needn't handle non-finite values.
Results may differ from a plain program's by a relative error of at most 0.004.
Values may be sent and summed in bfloat16 or wider, within the bound.
A program may use at most 64 MiB of HBM per device.

v0:
```python
import jax
import jax.numpy as jnp
from jax import lax
from jax.sharding import PartitionSpec as P

HEAD_DIM = 128


def absorb(partial_state, query_block, key_block, value_block):
    row_top, row_total, weighted = partial_state
    head_count = query_block.shape[1] // HEAD_DIM
    query_heads = query_block.reshape(query_block.shape[0], head_count, HEAD_DIM)
    key_heads = key_block.reshape(key_block.shape[0], head_count, HEAD_DIM)
    value_heads = value_block.reshape(value_block.shape[0], head_count, HEAD_DIM)
    scores = jnp.einsum(
        "qhd,khd->hqk", query_heads, key_heads, preferred_element_type=jnp.float32
    ) * HEAD_DIM ** (-0.5)
    new_top = jnp.maximum(row_top, jnp.max(scores, axis=2))
    shrink = jnp.exp(row_top - new_top)
    weights = jnp.exp(scores - new_top[:, :, None])
    row_total = row_total * shrink + jnp.sum(weights, axis=2)
    mixed_values = jnp.einsum(
        "hqk,khd->qhd",
        weights.astype(jnp.bfloat16),
        value_heads,
        preferred_element_type=jnp.float32,
    )
    weighted = weighted * jnp.transpose(shrink)[:, :, None] + mixed_values
    return (new_top, row_total, weighted)


def empty_state(row_count, columns):
    head_count = columns // HEAD_DIM
    return (
        jnp.full((head_count, row_count), -1e30, jnp.float32),
        jnp.zeros((head_count, row_count), jnp.float32),
        jnp.zeros((row_count, head_count, HEAD_DIM), jnp.float32),
    )


def finish(partial_state):
    row_top, row_total, weighted = partial_state
    normed = weighted / jnp.transpose(row_total)[:, :, None]
    return normed.reshape(weighted.shape[0], -1).astype(jnp.bfloat16)


def shards(enc_query, enc_key, enc_value, dec_query, cross_key, cross_value):
    local_query, local_key, local_value, visitor, resident_key, resident_value = (
        lax.all_to_all(enc_query, "tp", split_axis=1, concat_axis=0, tiled=True),
        lax.all_to_all(enc_key, "tp", split_axis=1, concat_axis=0, tiled=True),
        lax.all_to_all(enc_value, "tp", split_axis=1, concat_axis=0, tiled=True),
        lax.all_to_all(dec_query, "tp", split_axis=1, concat_axis=0, tiled=True),
        lax.all_to_all(cross_key, "tp", split_axis=1, concat_axis=0, tiled=True),
        lax.all_to_all(cross_value, "tp", split_axis=1, concat_axis=0, tiled=True),
    )
    enc_state = absorb(
        empty_state(local_query.shape[0], local_query.shape[1]),
        local_query,
        lax.all_gather(local_key, "ctx", axis=0, tiled=True),
        lax.all_gather(local_value, "ctx", axis=0, tiled=True),
    )
    enc_context = finish(enc_state)
    ring = lax.axis_size("ctx")
    rows, columns = visitor.shape
    heads = columns // HEAD_DIM
    every_query = lax.all_gather(visitor, "ctx", axis=0, tiled=True)
    row_top, row_total, weighted = absorb(
        empty_state(rows * ring, columns), every_query, resident_key, resident_value
    )
    stats = jnp.stack([row_top.T, row_total.T], axis=1).reshape(ring, rows, 2 * heads)
    sums = weighted.reshape(ring, rows, columns).astype(jnp.bfloat16)
    stats = lax.all_to_all(stats, "ctx", split_axis=0, concat_axis=0, tiled=True)
    sums = lax.all_to_all(sums, "ctx", split_axis=0, concat_axis=0, tiled=True)
    stats = stats.reshape(ring, rows, 2, heads)
    tops, totals = (stats[:, :, 0], stats[:, :, 1])
    scale = jnp.exp(tops - jnp.max(tops, axis=0, keepdims=True))
    total = jnp.sum(scale * totals, axis=0)
    mixed = jnp.sum(
        scale[..., None] * sums.reshape(ring, rows, heads, HEAD_DIM).astype(jnp.float32), axis=0
    )
    dec_context = (mixed / total[..., None]).reshape(rows, columns).astype(jnp.bfloat16)
    return (enc_context, dec_context)


def solution(mesh):
    in_specs = (
        P(("ctx", "tp"), None),
        P(("ctx", "tp"), None),
        P(("ctx", "tp"), None),
        P(("ctx", "tp"), None),
        P(("ctx", "tp"), None),
        P(("ctx", "tp"), None),
    )
    out_specs = (P("ctx", "tp"), P("ctx", "tp"))
    return jax.shard_map(shards, mesh=mesh, in_specs=in_specs, out_specs=out_specs, check_vma=False)
```

profile of v0, /device:TPU:1, one launch (start us, length us, event | category | flops | bytes accessed | tf_op | source)
XLA Modules:
  0.0 264.9 jit_solution(9463373634563402771)
XLA Ops:
  7.2 1.0 copy.75
  8.3 18.6 %all_to_all.115 = bf16[10,16,384]{2,0,1:T(8,128)(2,1)S(1)} all-to-all(bf16[10,16,384]{2,0,1:T(8,128)(2,1)S(1)} %copy.50), channel_id=1, replica_groups=mesh['ctx'=32,'tp'=16] {'tp'}, dimensions={1} | all-to-all | bytes 245760 | tf_op jit(solution)/shard_map/all_to_all | solution.py:50
  27.7 1.0 copy.76
  28.7 12.5 %all_to_all.116 = bf16[10,16,384]{2,0,1:T(8,128)(2,1)S(1)} all-to-all(bf16[10,16,384]{2,0,1:T(8,128)(2,1)S(1)} %copy.54), channel_id=1, replica_groups=mesh['ctx'=32,'tp'=16] {'tp'}, dimensions={1} | all-to-all | bytes 245760 | tf_op jit(solution)/shard_map/all_to_all | solution.py:51
  41.9 4.2 %all-to-all-start.3 = ((bf16[2,16,384]{2,0,1:T(2,128)(2,1)}), bf16[2,16,384]{2,0,1:T(2,128)(2,1)S(1)}, u32[]{:S(2)}, u32[]{:S(2)}) async-start(bf16[2,16,384]{2,0,1:T(2,128)(2,1)} %bitcast.118), calls=%async_computation.3 | async-start | bytes 49152 | tf_op jit(solution)/shard_map/all_to_all | solution.py:52
  46.1 1.0 copy.77
  49.3 3.8 %all-to-all-done.3 = bf16[2,16,384]{2,0,1:T(2,128)(2,1)S(1)} async-done(((bf16[2,16,384]{2,0,1:T(2,128)(2,1)}), bf16[2,16,384]{2,0,1:T(2,128)(2,1)S(1)}, u32[]{:S(2)}, u32[]{:S(2)}) %all-to-all-start.3) | async-done | bytes 24608 | tf_op jit(solution)/shard_map/all_to_all | solution.py:52
  53.1 3.5 %all-to-all-start.4 = ((bf16[10,16,384]{2,0,1:T(8,128)(2,1)}), bf16[10,16,384]{2,0,1:T(8,128)(2,1)S(1)}, u32[]{:S(2)}, u32[]{:S(2)}) async-start(bf16[10,16,384]{2,0,1:T(8,128)(2,1)} %copy.60), calls=%async_computation.4 | async-start | bytes 393216 | tf_op jit(solution)/shard_map/all_to_all | solution.py:53
  56.7 61.8 %all_gather.11 = bf16[1024,384]{1,0:T(8,128)(2,1)S(1)} all-gather(bf16[32,384]{1,0:T(8,128)(2,1)S(1)} %all_to_all.98), channel_id=1, replica_groups=mesh['ctx'=32,'tp'=16] {'ctx'}, dimensions={0}, use_global_device_ids=true | all-gather | bytes 811008 | tf_op jit(solution)/shard_map/all_gather | solution.py:66
  118.8 6.6 %all-to-all-start.6 = ((bf16[10,16,384]{2,0,1:T(8,128)(2,1)}), bf16[10,16,384]{2,0,1:T(8,128)(2,1)S(1)}, u32[]{:S(2)}, u32[]{:S(2)}) async-start(bf16[10,16,384]{2,0,1:T(8,128)(2,1)} %copy.66), calls=%async_computation.6 | async-start | bytes 393216 | tf_op jit(solution)/shard_map/all_to_all | solution.py:54
  126.3 8.1 %all-to-all-done.6 = bf16[10,16,384]{2,0,1:T(8,128)(2,1)S(1)} async-done(((bf16[10,16,384]{2,0,1:T(8,128)(2,1)}), bf16[10,16,384]{2,0,1:T(8,128)(2,1)S(1)}, u32[]{:S(2)}, u32[]{:S(2)}) %all-to-all-start.6) | async-done | bytes 122912 | tf_op jit(solution)/shard_map/all_to_all | solution.py:54
  134.4 3.9 %all-to-all-start = ((bf16[10,16,384]{2,0,1:T(8,128)(2,1)}), bf16[10,16,384]{2,0,1:T(8,128)(2,1)S(1)}, u32[]{:S(2)}, u32[]{:S(2)}) async-start(bf16[10,16,384]{2,0,1:T(8,128)(2,1)} %copy.49), calls=%async_computation | async-start | bytes 393216 | tf_op jit(solution)/shard_map/all_to_all | solution.py:49
  138.5 0.7 reshape.85
  139.3 7.3 %all-to-all-done = bf16[10,16,384]{2,0,1:T(8,128)(2,1)S(1)} async-done(((bf16[10,16,384]{2,0,1:T(8,128)(2,1)}), bf16[10,16,384]{2,0,1:T(8,128)(2,1)S(1)}, u32[]{:S(2)}, u32[]{:S(2)}) %all-to-all-start) | async-done | bytes 122912 | tf_op jit(solution)/shard_map/all_to_all | solution.py:49
  146.6 5.8 %all-to-all-start.5 = ((f32[32,1,192]{2,1,0:T(1,128)}), f32[32,1,192]{2,1,0:T(1,128)S(1)}, u32[]{:S(2)}, u32[]{:S(2)}) async-start(f32[32,1,192]{2,1,0:T(1,128)} %reshape.85), calls=%async_computation.5 | async-start | bytes 65536 | tf_op jit(solution)/shard_map/all_to_all | solution.py:72
  152.4 1.0 fusion.8
  154.1 1.4 convert_element_type.30
  155.5 8.8 %all-to-all-done.5 = f32[32,1,192]{2,1,0:T(1,128)S(1)} async-done(((f32[32,1,192]{2,1,0:T(1,128)}), f32[32,1,192]{2,1,0:T(1,128)S(1)}, u32[]{:S(2)}, u32[]{:S(2)}) %all-to-all-start.5) | async-done | bytes 24608 | tf_op jit(solution)/shard_map/all_to_all | solution.py:72
  164.3 4.6 %all-to-all-start.7 = ((bf16[32,32,384]{2,1,0:T(8,128)(2,1)}), bf16[32,32,384]{2,1,0:T(8,128)(2,1)S(1)}, u32[]{:S(2)}, u32[]{:S(2)}) async-start(bf16[32,32,384]{2,1,0:T(8,128)(2,1)} %convert_element_type.30), calls=%async_computation.7 | async-start | bytes 1572864 | tf_op jit(solution)/shard_map/all_to_all | solution.py:73
  168.9 0.7 reshape.77
  170.2 0.7 reduce.2
  171.4 1.2 mul.41
  172.6 1.8 mul.42
  174.5 20.3 %all-to-all-done.7 = bf16[32,32,384]{2,1,0:T(8,128)(2,1)S(1)} async-done(((bf16[32,32,384]{2,1,0:T(8,128)(2,1)}), bf16[32,32,384]{2,1,0:T(8,128)(2,1)S(1)}, u32[]{:S(2)}, u32[]{:S(2)}) %all-to-all-start.7) | async-done | bytes 786464 | tf_op jit(solution)/shard_map/all_to_all | solution.py:73
  194.8 1.6 multiply_reduce_fusion.2
  197.1 6.3 %copy.51 = bf16[5120,384]{0,1:T(8,128)(2,1)} copy(bf16[5120,384]{1,0:T(8,128)(2,1)} %all-gather.3.cloned.1.call-done) | data formatting | bytes 7864320 | tf_op jit(solution)/shard_map/all_gather | solution.py:59
  203.4 3.6 %multiply_reduce_fusion = (f32[3,160]{1,0:T(4,128)S(1)}, f32[3,160,5120]{2,1,0:T(8,128)S(1)}) fusion(bf16[5120,3,128]{0,2,1:T(8,128)(2,1)} %bitcast.93, bf16[160,3,128]{2,1,0:T(4,128)(2,1)S(1)} %copy-done.1), kind=kOutput, calls=%fused_computation.1 | convolution fusion | flops 634060288 | bytes 13887360 | tf_op jit(solution)/shard_map/qhd,khd->hqk/dot_general | solution.py:15
  207.1 1.8 fusion
  208.9 2.0 copy-done
  210.9 33.3 %all-gather.5.cloned.1.call-done = bf16[5120,384]{1,0:T(8,128)(2,1)} async-done(((bf16[160,384]{1,0:T(8,128)(2,1)}), bf16[5120,384]{1,0:T(8,128)(2,1)}) %all-gather.5.cloned.1.call-update) | async-done | bytes 3932176 | tf_op jit(solution)/shard_map/all_gather | solution.py:60
  244.2 6.3 %copy.55 = bf16[5120,384]{0,1:T(8,128)(2,1)} copy(bf16[5120,384]{1,0:T(8,128)(2,1)} %all-gather.5.cloned.1.call-done) | data formatting | bytes 7864320 | tf_op jit(solution)/shard_map/all_gather | solution.py:60
  250.5 6.9 %fusion.21 = bf16[3,20,8,128]{3,2,1,0:T(8,128)(2,1)S(1)} fusion(bf16[5120,3,128]{0,2,1:T(8,128)(2,1)} %bitcast.94, f32[3,160,5120]{2,1,0:T(8,128)} %copy-done, f32[3,160]{1,0:T(4,128)S(1)} %get-tuple-element.9, f32[160,3]{0,1:T(4,128)S(1)} %bitcast_add_fusion.2, f32[160,3]{0,1:T(4,128)S(1)} %get-tuple-element.8), kind=kOutput, calls=%fused_computation.18 | convolution fusion | flops 636702720 | bytes 13891200 | tf_op jit(solution)/shard_map/hqk,khd->qhd/dot_general | solution.py:22
  (51 shorter events, 8.4 us)
Async XLA Ops:
  7.2 40.6 %copy-start.2 = (bf16[10,6144]{1,0:T(8,128)(2,1)S(1)}, bf16[10,6144]{1,0:T(8,128)(2,1)}, u32[]{:S(2)}) copy-start(bf16[10,6144]{1,0:T(8,128)(2,1)} %param.11) | copy-start | bytes 368644
  7.2 41.4 %copy-start.3 = (bf16[10,6144]{1,0:T(8,128)(2,1)S(1)}, bf16[10,6144]{1,0:T(8,128)(2,1)}, u32[]{:S(2)}) copy-start(bf16[10,6144]{1,0:T(8,128)(2,1)} %param.6) | copy-start | bytes 368644
  7.2 189.9 %all-gather.3.cloned.1.call-start = ((), (), s32[]{:S(2)}) async-start(), calls=%async_computation.8 | async-start | bytes 4055040 | tf_op jit(solution)/shard_map/all_gather | solution.py:59
  27.7 216.5 %all-gather.5.cloned.1.call-start = ((), (), s32[]{:S(2)}) async-start(), calls=%async_computation.9 | async-start | bytes 4055040 | tf_op jit(solution)/shard_map/all_gather | solution.py:60
  41.9 11.2 %all-to-all-start.3 = ((bf16[2,16,384]{2,0,1:T(2,128)(2,1)}), bf16[2,16,384]{2,0,1:T(2,128)(2,1)S(1)}, u32[]{:S(2)}, u32[]{:S(2)}) async-start(bf16[2,16,384]{2,0,1:T(2,128)(2,1)} %bitcast.118), calls=%async_computation.3 | async-start | bytes 49152 | tf_op jit(solution)/shard_map/all_to_all | solution.py:52
  53.1 65.7 %all-to-all-start.4 = ((bf16[10,16,384]{2,0,1:T(8,128)(2,1)}), bf16[10,16,384]{2,0,1:T(8,128)(2,1)S(1)}, u32[]{:S(2)}, u32[]{:S(2)}) async-start(bf16[10,16,384]{2,0,1:T(8,128)(2,1)} %copy.60), calls=%async_computation.4 | async-start | bytes 393216 | tf_op jit(solution)/shard_map/all_to_all | solution.py:53
  118.8 15.6 %all-to-all-start.6 = ((bf16[10,16,384]{2,0,1:T(8,128)(2,1)}), bf16[10,16,384]{2,0,1:T(8,128)(2,1)S(1)}, u32[]{:S(2)}, u32[]{:S(2)}) async-start(bf16[10,16,384]{2,0,1:T(8,128)(2,1)} %copy.66), calls=%async_computation.6 | async-start | bytes 393216 | tf_op jit(solution)/shard_map/all_to_all | solution.py:54
  134.4 12.2 %all-to-all-start = ((bf16[10,16,384]{2,0,1:T(8,128)(2,1)}), bf16[10,16,384]{2,0,1:T(8,128)(2,1)S(1)}, u32[]{:S(2)}, u32[]{:S(2)}) async-start(bf16[10,16,384]{2,0,1:T(8,128)(2,1)} %copy.49), calls=%async_computation | async-start | bytes 393216 | tf_op jit(solution)/shard_map/all_to_all | solution.py:49
  146.6 17.8 %all-to-all-start.5 = ((f32[32,1,192]{2,1,0:T(1,128)}), f32[32,1,192]{2,1,0:T(1,128)S(1)}, u32[]{:S(2)}, u32[]{:S(2)}) async-start(f32[32,1,192]{2,1,0:T(1,128)} %reshape.85), calls=%async_computation.5 | async-start | bytes 65536 | tf_op jit(solution)/shard_map/all_to_all | solution.py:72
  164.3 30.5 %all-to-all-start.7 = ((bf16[32,32,384]{2,1,0:T(8,128)(2,1)}), bf16[32,32,384]{2,1,0:T(8,128)(2,1)S(1)}, u32[]{:S(2)}, u32[]{:S(2)}) async-start(bf16[32,32,384]{2,1,0:T(8,128)(2,1)} %convert_element_type.30), calls=%async_computation.7 | async-start | bytes 1572864 | tf_op jit(solution)/shard_map/all_to_all | solution.py:73
  197.1 6.3 %copy-start.1 = (bf16[160,3,128]{2,1,0:T(4,128)(2,1)S(1)}, bf16[160,3,128]{2,1,0:T(4,128)(2,1)}, u32[]{:S(2)}) copy-start(bf16[160,3,128]{2,1,0:T(4,128)(2,1)} %reshape.77) | copy-start | bytes 368644
  207.1 3.8 %copy-start = (f32[3,160,5120]{2,1,0:T(8,128)}, f32[3,160,5120]{2,1,0:T(8,128)S(1)}, u32[]{:S(2)}) copy-start(f32[3,160,5120]{2,1,0:T(8,128)S(1)} %get-tuple-element.11) | copy-start | bytes 29491204
Sparse Core Ops, SparseCore 0:
  27.8 109.4 all-gather.2
  141.2 102.8 all-gather.4
where the time goes:
time: 266 us; the launch traced here: 265 us
  blocking collectives  92.9 us (35%)
  waiting for transfers between devices  81.7 us (31%)
  local copies, waits for them, and re-layouts  30.2 us (11%)
  starting transfers between devices  28.6 us (11%)
  between operations  14.3 us (5%)
  matrix products  12 us (5%)
  other arithmetic  5.18 us (2%)
    all_gather x1, blocking collectives, shards(): every_query = lax.all_gather(visitor, 'ctx', axis=0, tiled=True)  61.8 us
    all_gather x1, waiting for transfers between devices, shards(): lax.all_gather(local_value, 'ctx', axis=0, tiled=True)  33.3 us
    all_to_all x1, waiting for transfers between devices, shards(): sums = lax.all_to_all(sums, 'ctx', split_axis=0, concat_axis=0, tiled=True)  20.3 us
    all_to_all x1, blocking collectives, shards(): lax.all_to_all(enc_key, 'tp', split_axis=1, concat_axis=0, tiled=True)  18.6 us
    all_to_all x1, blocking collectives, shards(): lax.all_to_all(enc_value, 'tp', split_axis=1, concat_axis=0, tiled=True)  12.5 us
    all_to_all x1, waiting for transfers between devices, shards(): lax.all_to_all(stats, 'ctx', split_axis=0, concat_axis=0, tiled=True)  8.81 us
    all_to_all x1, waiting for transfers between devices, shards(): lax.all_to_all(cross_value, 'tp', split_axis=1, concat_axis=0, tiled=True)  8.13 us
    dot_general x2, matrix products, absorb(): jnp.einsum('hqk,khd->qhd', weights.astype(jnp.bfloat16), value_heads, pre...  7.91 us
  transfers between devices with their start and end apart: 8, of which 6 were waited for; matrix products, arithmetic and copies ran while one was open for 11% of the time, Pallas kernels for 0%

commit v1 on v0

--- a/solution.py
+++ b/solution.py
@@ -63,7 +63,9 @@
     ring = lax.axis_size("ctx")
     rows, columns = visitor.shape
     heads = columns // HEAD_DIM
-    every_query = lax.all_gather(visitor, "ctx", axis=0, tiled=True)
+    every_query = jnp.concatenate(
+        lax.all_to_all(jnp.stack([visitor] * lax.axis_size("ctx")), "ctx", 0, 0), axis=0
+    )
     row_top, row_total, weighted = absorb(
         empty_state(rows * ring, columns), every_query, resident_key, resident_value
     )

time: 266 us -> 286 us (1.075)
  blocking collectives: 92.9 us -> 31.2 us
  waiting for transfers between devices: 81.7 us -> 143 us
  starting transfers between devices: 28.6 us -> 47.6 us
    all_gather x1 -> x0, blocking collectives: 61.8 us -> none  [shards(): every_query = lax.all_gather(visitor, 'ctx', axis=0, tiled=True)]
    all_gather x1, waiting for transfers between devices: 33.3 us -> 59.5 us  [shards(): lax.all_gather(local_value, 'ctx', axis=0, tiled=True)]
    all_to_all x0 -> x1, waiting for transfers between devices: none -> 24.9 us  [shards(): lax.all_to_all(jnp.stack([visitor] * lax.axis_size('ctx')), 'ctx', 0, 0)]
    all_to_all x0 -> x1, starting transfers between devices: none -> 18 us  [shards(): lax.all_to_all(jnp.stack([visitor] * lax.axis_size('ctx')), 'ctx', 0, 0)]
    all_to_all x1, waiting for transfers between devices: 0.01 us -> 7.51 us  [shards(): lax.all_to_all(cross_key, 'tp', split_axis=1, concat_axis=0, tiled=True)]
    all_to_all x1, starting transfers between devices: 5.8 us -> 9.07 us  [shards(): lax.all_to_all(stats, 'ctx', split_axis=0, concat_axis=0, tiled=True)]
    all_to_all x1, starting transfers between devices: 6.58 us -> 3.52 us  [shards(): lax.all_to_all(cross_value, 'tp', split_axis=1, concat_axis=0, tiled=True)]
  transfers between devices with their start and end apart: 8 -> 9, of which waited for: 6 -> 8; matrix products, arithmetic and copies ran while one was open for 11% -> 11% of each run, Pallas kernels for 0% -> 0%
where the time goes in v1:
time: 286 us; the launch traced here: 284 us
  waiting for transfers between devices  143 us (50%)
  starting transfers between devices  47.6 us (17%)
  local copies, waits for them, and re-layouts  31.2 us (11%)
  blocking collectives  31.2 us (11%)
  between operations  14.4 us (5%)
  matrix products  12 us (4%)
  other arithmetic  5.18 us (2%)
    all_gather x1, waiting for transfers between devices, shards(): lax.all_gather(local_value, 'ctx', axis=0, tiled=True)  59.5 us
    all_to_all x1, waiting for transfers between devices, shards(): lax.all_to_all(jnp.stack([visitor] * lax.axis_size('ctx')), 'ctx', 0, 0)  24.9 us
    all_to_all x1, waiting for transfers between devices, shards(): sums = lax.all_to_all(sums, 'ctx', split_axis=0, concat_axis=0, tiled=True)  22.4 us
    all_to_all x1, blocking collectives, shards(): lax.all_to_all(enc_key, 'tp', split_axis=1, concat_axis=0, tiled=True)  18.7 us
    all_to_all x1, starting transfers between devices, shards(): lax.all_to_all(jnp.stack([visitor] * lax.axis_size('ctx')), 'ctx', 0, 0)  18 us
    all_to_all x1, blocking collectives, shards(): lax.all_to_all(enc_value, 'tp', split_axis=1, concat_axis=0, tiled=True)  12.5 us
    all_to_all x1, starting transfers between devices, shards(): lax.all_to_all(stats, 'ctx', split_axis=0, concat_axis=0, tiled=True)  9.07 us
    all_to_all x1, waiting for transfers between devices, shards(): lax.all_to_all(stats, 'ctx', split_axis=0, concat_axis=0, tiled=True)  8.69 us
  transfers between devices with their start and end apart: 9, of which 8 were waited for; matrix products, arithmetic and copies ran while one was open for 11% of the time, Pallas kernels for 0%

profile of v1, /device:TPU:1, one launch (start us, length us, event | category | flops | bytes accessed | tf_op | source)
XLA Modules:
  0.0 284.5 jit_solution(14197736209707425150)
XLA Ops:
  7.2 1.0 copy.71
  8.3 18.7 %all_to_all.117 = bf16[10,16,384]{2,0,1:T(8,128)(2,1)S(1)} all-to-all(bf16[10,16,384]{2,0,1:T(8,128)(2,1)S(1)} %copy.48), channel_id=1, replica_groups=mesh['ctx'=32,'tp'=16] {'tp'}, dimensions={1} | all-to-all | bytes 245760 | tf_op jit(solution)/shard_map/all_to_all | solution.py:50
  27.8 1.0 copy.72
  28.8 12.5 %all_to_all.118 = bf16[10,16,384]{2,0,1:T(8,128)(2,1)S(1)} all-to-all(bf16[10,16,384]{2,0,1:T(8,128)(2,1)S(1)} %copy.52), channel_id=1, replica_groups=mesh['ctx'=32,'tp'=16] {'tp'}, dimensions={1} | all-to-all | bytes 245760 | tf_op jit(solution)/shard_map/all_to_all | solution.py:51
  42.0 4.2 %all-to-all-start.3 = ((bf16[2,16,384]{2,0,1:T(2,128)(2,1)}), bf16[2,16,384]{2,0,1:T(2,128)(2,1)S(1)}, u32[]{:S(2)}, u32[]{:S(2)}) async-start(bf16[2,16,384]{2,0,1:T(2,128)(2,1)} %bitcast.115), calls=%async_computation.3 | async-start | bytes 49152 | tf_op jit(solution)/shard_map/all_to_all | solution.py:52
  46.2 1.0 copy.73
  47.9 5.4 %all-to-all-done.3 = bf16[2,16,384]{2,0,1:T(2,128)(2,1)S(1)} async-done(((bf16[2,16,384]{2,0,1:T(2,128)(2,1)}), bf16[2,16,384]{2,0,1:T(2,128)(2,1)S(1)}, u32[]{:S(2)}, u32[]{:S(2)}) %all-to-all-start.3) | async-done | bytes 24608 | tf_op jit(solution)/shard_map/all_to_all | solution.py:52
  53.2 3.5 %all-to-all-start.5 = ((bf16[10,16,384]{2,0,1:T(8,128)(2,1)}), bf16[10,16,384]{2,0,1:T(8,128)(2,1)S(1)}, u32[]{:S(2)}, u32[]{:S(2)}) async-start(bf16[10,16,384]{2,0,1:T(8,128)(2,1)} %copy.57), calls=%async_computation.5 | async-start | bytes 393216 | tf_op jit(solution)/shard_map/all_to_all | solution.py:53
  57.5 7.5 %all-to-all-done.5 = bf16[10,16,384]{2,0,1:T(8,128)(2,1)S(1)} async-done(((bf16[10,16,384]{2,0,1:T(8,128)(2,1)}), bf16[10,16,384]{2,0,1:T(8,128)(2,1)S(1)}, u32[]{:S(2)}, u32[]{:S(2)}) %all-to-all-start.5) | async-done | bytes 122912 | tf_op jit(solution)/shard_map/all_to_all | solution.py:53
  65.0 3.5 %all-to-all-start.7 = ((bf16[10,16,384]{2,0,1:T(8,128)(2,1)}), bf16[10,16,384]{2,0,1:T(8,128)(2,1)S(1)}, u32[]{:S(2)}, u32[]{:S(2)}) async-start(bf16[10,16,384]{2,0,1:T(8,128)(2,1)} %copy.63), calls=%async_computation.7 | async-start | bytes 393216 | tf_op jit(solution)/shard_map/all_to_all | solution.py:54
  68.6 8.2 %all-to-all-done.7 = bf16[10,16,384]{2,0,1:T(8,128)(2,1)S(1)} async-done(((bf16[10,16,384]{2,0,1:T(8,128)(2,1)}), bf16[10,16,384]{2,0,1:T(8,128)(2,1)S(1)}, u32[]{:S(2)}, u32[]{:S(2)}) %all-to-all-start.7) | async-done | bytes 122912 | tf_op jit(solution)/shard_map/all_to_all | solution.py:54
  76.8 1.0 stack.11
  77.8 18.0 %all-to-all-start.4 = ((bf16[32,32,384]{2,1,0:T(8,128)(2,1)}), bf16[32,32,384]{2,1,0:T(8,128)(2,1)S(1)}, u32[]{:S(2)}, u32[]{:S(2)}) async-start(bf16[32,32,384]{2,1,0:T(8,128)(2,1)} %stack.11), calls=%async_computation.4 | async-start | bytes 1572864 | tf_op jit(solution)/shard_map/all_to_all | solution.py:67
  96.7 24.9 %all-to-all-done.4 = bf16[32,32,384]{2,1,0:T(8,128)(2,1)S(1)} async-done(((bf16[32,32,384]{2,1,0:T(8,128)(2,1)}), bf16[32,32,384]{2,1,0:T(8,128)(2,1)S(1)}, u32[]{:S(2)}, u32[]{:S(2)}) %all-to-all-start.4) | async-done | bytes 786464 | tf_op jit(solution)/shard_map/all_to_all | solution.py:67
  121.7 4.7 %all-to-all-start = ((bf16[10,16,384]{2,0,1:T(8,128)(2,1)}), bf16[10,16,384]{2,0,1:T(8,128)(2,1)S(1)}, u32[]{:S(2)}, u32[]{:S(2)}) async-start(bf16[10,16,384]{2,0,1:T(8,128)(2,1)} %copy.47), calls=%async_computation | async-start | bytes 393216 | tf_op jit(solution)/shard_map/all_to_all | solution.py:49
  128.4 6.3 %all-to-all-done = bf16[10,16,384]{2,0,1:T(8,128)(2,1)S(1)} async-done(((bf16[10,16,384]{2,0,1:T(8,128)(2,1)}), bf16[10,16,384]{2,0,1:T(8,128)(2,1)S(1)}, u32[]{:S(2)}, u32[]{:S(2)}) %all-to-all-start) | async-done | bytes 122912 | tf_op jit(solution)/shard_map/all_to_all | solution.py:49
  134.7 9.1 %all-to-all-start.6 = ((f32[32,1,192]{2,1,0:T(1,128)}), f32[32,1,192]{2,1,0:T(1,128)S(1)}, u32[]{:S(2)}, u32[]{:S(2)}) async-start(f32[32,1,192]{2,1,0:T(1,128)} %reshape.84), calls=%async_computation.6 | async-start | bytes 65536 | tf_op jit(solution)/shard_map/all_to_all | solution.py:74
  143.8 1.0 fusion.8
  145.5 1.4 convert_element_type.30
  146.9 8.7 %all-to-all-done.6 = f32[32,1,192]{2,1,0:T(1,128)S(1)} async-done(((f32[32,1,192]{2,1,0:T(1,128)}), f32[32,1,192]{2,1,0:T(1,128)S(1)}, u32[]{:S(2)}, u32[]{:S(2)}) %all-to-all-start.6) | async-done | bytes 24608 | tf_op jit(solution)/shard_map/all_to_all | solution.py:74
  155.6 4.5 %all-to-all-start.8 = ((bf16[32,32,384]{2,1,0:T(8,128)(2,1)}), bf16[32,32,384]{2,1,0:T(8,128)(2,1)S(1)}, u32[]{:S(2)}, u32[]{:S(2)}) async-start(bf16[32,32,384]{2,1,0:T(8,128)(2,1)} %convert_element_type.30), calls=%async_computation.8 | async-start | bytes 1572864 | tf_op jit(solution)/shard_map/all_to_all | solution.py:75
  162.5 1.2 mul.41
  163.7 1.8 mul.42
  165.6 22.4 %all-to-all-done.8 = bf16[32,32,384]{2,1,0:T(8,128)(2,1)S(1)} async-done(((bf16[32,32,384]{2,1,0:T(8,128)(2,1)}), bf16[32,32,384]{2,1,0:T(8,128)(2,1)S(1)}, u32[]{:S(2)}, u32[]{:S(2)}) %all-to-all-start.8) | async-done | bytes 786464 | tf_op jit(solution)/shard_map/all_to_all | solution.py:75
  188.0 1.6 multiply_reduce_fusion.2
  190.4 6.4 %copy.49 = bf16[5120,384]{0,1:T(8,128)(2,1)} copy(bf16[5120,384]{1,0:T(8,128)(2,1)} %all-gather.3.cloned.1.call-done) | data formatting | bytes 7864320 | tf_op jit(solution)/shard_map/all_gather | solution.py:59
  196.7 3.7 %multiply_reduce_fusion = (f32[3,160]{1,0:T(4,128)S(1)}, f32[3,160,5120]{2,1,0:T(8,128)S(1)}) fusion(bf16[5120,3,128]{0,2,1:T(8,128)(2,1)} %bitcast.91, bf16[160,3,128]{2,1,0:T(4,128)(2,1)S(1)} %copy-done.1), kind=kOutput, calls=%fused_computation.1 | convolution fusion | flops 634060288 | bytes 13887360 | tf_op jit(solution)/shard_map/qhd,khd->hqk/dot_general | solution.py:15
  200.4 1.8 fusion
  202.2 2.0 copy-done
  204.2 59.5 %all-gather.5.cloned.1.call-done = bf16[5120,384]{1,0:T(8,128)(2,1)} async-done(((bf16[160,384]{1,0:T(8,128)(2,1)}), bf16[5120,384]{1,0:T(8,128)(2,1)}) %all-gather.5.cloned.1.call-update) | async-done | bytes 3932176 | tf_op jit(solution)/shard_map/all_gather | solution.py:60
  263.7 6.4 %copy.53 = bf16[5120,384]{0,1:T(8,128)(2,1)} copy(bf16[5120,384]{1,0:T(8,128)(2,1)} %all-gather.5.cloned.1.call-done) | data formatting | bytes 7864320 | tf_op jit(solution)/shard_map/all_gather | solution.py:60
  270.0 6.9 %fusion.21 = bf16[3,20,8,128]{3,2,1,0:T(8,128)(2,1)S(1)} fusion(bf16[5120,3,128]{0,2,1:T(8,128)(2,1)} %bitcast.92, f32[3,160,5120]{2,1,0:T(8,128)} %copy-done, f32[3,160]{1,0:T(4,128)S(1)} %get-tuple-element.9, f32[160,3]{0,1:T(4,128)S(1)} %bitcast_add_fusion.2, f32[160,3]{0,1:T(4,128)S(1)} %get-tuple-element.8), kind=kOutput, calls=%fused_computation.18 | convolution fusion | flops 636702720 | bytes 13891200 | tf_op jit(solution)/shard_map/hqk,khd->qhd/dot_general | solution.py:22
  (53 shorter events, 10.5 us)
Async XLA Ops:
  7.2 49.6 %copy-start.2 = (bf16[10,6144]{1,0:T(8,128)(2,1)S(1)}, bf16[10,6144]{1,0:T(8,128)(2,1)}, u32[]{:S(2)}) copy-start(bf16[10,6144]{1,0:T(8,128)(2,1)} %param.11) | copy-start | bytes 368644
  7.2 183.2 %all-gather.3.cloned.1.call-start = ((), (), s32[]{:S(2)}) async-start(), calls=%async_computation.9 | async-start | bytes 4055040 | tf_op jit(solution)/shard_map/all_gather | solution.py:59
  8.3 87.6 %copy-start.3 = (bf16[10,6144]{1,0:T(8,128)(2,1)S(1)}, bf16[10,6144]{1,0:T(8,128)(2,1)}, u32[]{:S(2)}) copy-start(bf16[10,6144]{1,0:T(8,128)(2,1)} %param.6) | copy-start | bytes 368644
  27.8 235.9 %all-gather.5.cloned.1.call-start = ((), (), s32[]{:S(2)}) async-start(), calls=%async_computation.10 | async-start | bytes 4055040 | tf_op jit(solution)/shard_map/all_gather | solution.py:60
  42.0 11.2 %all-to-all-start.3 = ((bf16[2,16,384]{2,0,1:T(2,128)(2,1)}), bf16[2,16,384]{2,0,1:T(2,128)(2,1)S(1)}, u32[]{:S(2)}, u32[]{:S(2)}) async-start(bf16[2,16,384]{2,0,1:T(2,128)(2,1)} %bitcast.115), calls=%async_computation.3 | async-start | bytes 49152 | tf_op jit(solution)/shard_map/all_to_all | solution.py:52
  53.2 11.8 %all-to-all-start.5 = ((bf16[10,16,384]{2,0,1:T(8,128)(2,1)}), bf16[10,16,384]{2,0,1:T(8,128)(2,1)S(1)}, u32[]{:S(2)}, u32[]{:S(2)}) async-start(bf16[10,16,384]{2,0,1:T(8,128)(2,1)} %copy.57), calls=%async_computation.5 | async-start | bytes 393216 | tf_op jit(solution)/shard_map/all_to_all | solution.py:53
  65.0 11.8 %all-to-all-start.7 = ((bf16[10,16,384]{2,0,1:T(8,128)(2,1)}), bf16[10,16,384]{2,0,1:T(8,128)(2,1)S(1)}, u32[]{:S(2)}, u32[]{:S(2)}) async-start(bf16[10,16,384]{2,0,1:T(8,128)(2,1)} %copy.63), calls=%async_computation.7 | async-start | bytes 393216 | tf_op jit(solution)/shard_map/all_to_all | solution.py:54
  77.8 43.9 %all-to-all-start.4 = ((bf16[32,32,384]{2,1,0:T(8,128)(2,1)}), bf16[32,32,384]{2,1,0:T(8,128)(2,1)S(1)}, u32[]{:S(2)}, u32[]{:S(2)}) async-start(bf16[32,32,384]{2,1,0:T(8,128)(2,1)} %stack.11), calls=%async_computation.4 | async-start | bytes 1572864 | tf_op jit(solution)/shard_map/all_to_all | solution.py:67
  121.7 13.0 %all-to-all-start = ((bf16[10,16,384]{2,0,1:T(8,128)(2,1)}), bf16[10,16,384]{2,0,1:T(8,128)(2,1)S(1)}, u32[]{:S(2)}, u32[]{:S(2)}) async-start(bf16[10,16,384]{2,0,1:T(8,128)(2,1)} %copy.47), calls=%async_computation | async-start | bytes 393216 | tf_op jit(solution)/shard_map/all_to_all | solution.py:49
  134.7 20.9 %all-to-all-start.6 = ((f32[32,1,192]{2,1,0:T(1,128)}), f32[32,1,192]{2,1,0:T(1,128)S(1)}, u32[]{:S(2)}, u32[]{:S(2)}) async-start(f32[32,1,192]{2,1,0:T(1,128)} %reshape.84), calls=%async_computation.6 | async-start | bytes 65536 | tf_op jit(solution)/shard_map/all_to_all | solution.py:74
  155.6 32.5 %all-to-all-start.8 = ((bf16[32,32,384]{2,1,0:T(8,128)(2,1)}), bf16[32,32,384]{2,1,0:T(8,128)(2,1)S(1)}, u32[]{:S(2)}, u32[]{:S(2)}) async-start(bf16[32,32,384]{2,1,0:T(8,128)(2,1)} %convert_element_type.30), calls=%async_computation.8 | async-start | bytes 1572864 | tf_op jit(solution)/shard_map/all_to_all | solution.py:75
  190.4 6.4 %copy-start.1 = (bf16[160,3,128]{2,1,0:T(4,128)(2,1)S(1)}, bf16[160,3,128]{2,1,0:T(4,128)(2,1)}, u32[]{:S(2)}) copy-start(bf16[160,3,128]{2,1,0:T(4,128)(2,1)} %reshape.77) | copy-start | bytes 368644
  200.4 3.8 %copy-start = (f32[3,160,5120]{2,1,0:T(8,128)}, f32[3,160,5120]{2,1,0:T(8,128)S(1)}, u32[]{:S(2)}) copy-start(f32[3,160,5120]{2,1,0:T(8,128)S(1)} %get-tuple-element.11) | copy-start | bytes 29491204
Sparse Core Ops, SparseCore 0:
  27.9 124.7 all-gather.2
  156.6 107.0 all-gather.4
